TPU v7x, 256 devices: a whole 4x4x8 slice. The times are simulated.
256 devices in a mesh: wide: 32 (over z, x), narrow: 8 (over y, core).
Axes of the slice: x: 4, y: 4, z: 8, core: 2. Of those that a mesh axis runs over, the one named last changes fastest.
Arguments:
- samples: bfloat16 [131072, 1024], P(('wide', 'narrow')), may hold values from -16 to 16
- centroid_table: bfloat16 [65536, 1024], P('wide', 'narrow'), may hold values from -6 to 6
- owner: int32 [65536], replicated, may hold values from 0 to 31, as said below
- slot: int32 [65536], replicated, may hold values from 0 to 2047, as said below
- assign: int32 [131072], P('wide'), may hold values from 0 to 65535, as said below
- codebook: float32 [8, 2048, 128], P('narrow'), may hold values from -16 to 16
Outputs:
- residual: bfloat16 [131072, 1024], P('wide', 'narrow')
- refined: float32 [8, 2048, 128], P('narrow')
Inputs may be any that keep to these rules, and one draw needn't show every extreme that they name: owner and slot give each coarse centroid a distinct storage position owner * 2048 + slot. `slot`: see owner. `assign`: in each aligned block of 4096 rows (the rows of one index of wide), at most 256 rows have centroids with one owner, and some owner has exactly 256.
All inputs are finite; a program needn't handle non-finite values.
Results may differ from a plain program's by a relative error of at most 0.0079.
Values may be sent and summed in bfloat16 or wider, within the bound.
A program may use at most 64 MiB of HBM per device.

v0:
```python
import jax
import jax.numpy as jnp
from jax import lax
from jax.sharding import PartitionSpec as P

ITERS = 2


softness_level = 16.0
prior_weight = 1.0


def cut_along(value, dim, count):
    shape = value.shape
    tiles = value.reshape(*shape[:dim], count, shape[dim] // count, *shape[dim + 1 :])
    return jnp.moveaxis(tiles, dim, 0)


def summed_on_arrival(value, axis, dim):
    count = lax.axis_size(axis)
    tiles = lax.all_to_all(cut_along(value, dim, count), axis, 0, 0, tiled=True)
    return jnp.sum(tiles, axis=0)


def padded_to(lines, count):
    spare = -len(lines) % count
    return jnp.pad(lines, [(0, spare)] + [(0, 0)] * (lines.ndim - 1))


def from_everyone(value, axis):
    count = lax.axis_size(axis)
    return lax.all_to_all(
        jnp.broadcast_to(value[None], (count, *value.shape)), axis, 0, 0, tiled=True
    )


def joined_along(tiles, dim):
    tiles = jnp.moveaxis(tiles, 0, dim)
    shape = tiles.shape
    return tiles.reshape(*shape[:dim], shape[dim] * shape[dim + 1], *shape[dim + 2 :])


def collect(value, axis, dim):
    tiles = from_everyone(value, axis)
    return joined_along(tiles, dim)


def sum_by_parts(value, axes):
    own = summed_on_arrival(padded_to(value, lax.axis_size(axes)), axes, 0)
    whole = collect(own, axes, 0)
    return whole[: len(value)].reshape(value.shape)


def in_one(arrays, axis):
    vector, at, outs = (jnp.concatenate([a.reshape(-1) for a in arrays]), 0, [])
    total = sum_by_parts(vector, axis)
    for a in arrays:
        outs.append(total[at : at + a.size].reshape(a.shape))
        at += a.size
    return tuple(outs)


def score_pass(blocks, narrow_words, codeword_norm_values):
    spaces = narrow_words.shape[0]
    words_count = narrow_words.shape[1]
    sub_width = narrow_words.shape[2]

    def block_step(running, row_block):
        inner_product_rows = jnp.einsum(
            "bms,mks->mbk", row_block, narrow_words, preferred_element_type=jnp.float32
        )
        score_matrix = (
            2.0 * inner_product_rows - codeword_norm_values[:, None, :]
        ) / softness_level
        weights_soft = jax.nn.softmax(score_matrix, axis=2).astype(jnp.bfloat16)
        totals = running[0] + jnp.einsum(
            "mbk,bms->mks", weights_soft, row_block, preferred_element_type=jnp.float32
        )
        return ((totals, running[1] + jnp.sum(weights_soft, axis=1, dtype=jnp.float32)), None)

    start = (
        jnp.zeros((spaces, words_count, sub_width), jnp.float32),
        jnp.zeros((spaces, words_count), jnp.float32),
    )
    (totals, counts), ignored = lax.scan(block_step, start, blocks)
    return (totals, counts)


def on_device(samples, centroid_table, owner, slot, assign, codebook):
    regrouped = lax.all_to_all(samples, "narrow", split_axis=1, concat_axis=0, tiled=True)
    group_rows = regrouped.shape[0]
    owner_of = owner[assign]
    slot_of = slot[assign]
    whole = lax.all_gather(centroid_table, "wide", axis=0, tiled=True)
    centre = jnp.take(whole, owner_of * centroid_table.shape[0] + slot_of, axis=0)
    residual = (regrouped.astype(jnp.float32) - centre.astype(jnp.float32)).astype(jnp.bfloat16)
    spaces = codebook.shape[0]
    sub_width = codebook.shape[2]
    block_size = 512
    blocks = residual.reshape(group_rows // block_size, block_size, spaces, sub_width)
    codewords = codebook
    narrow_words = codebook.astype(jnp.bfloat16)
    codeword_norm_values = jnp.sum(codebook * codebook, axis=2)
    for iteration in range(ITERS):
        narrow_words = codewords.astype(jnp.bfloat16)
        codeword_norm_values = jnp.sum(codewords * codewords, axis=2)
        totals, counts = score_pass(blocks, narrow_words, codeword_norm_values)
        totals, counts = in_one((totals, counts), "wide")
        codewords = (totals + prior_weight * codewords) / (counts[:, :, None] + prior_weight)
    return (residual, codewords)


def solution(mesh):
    return jax.shard_map(
        on_device,
        mesh=mesh,
        in_specs=(
            P(("wide", "narrow"), None),
            P("wide", "narrow"),
            P(),
            P(),
            P("wide"),
            P("narrow", None, None),
        ),
        out_specs=(P("wide", "narrow"), P("narrow", None, None)),
        check_vma=False,
    )
```

profile of v0, /device:TPU:2, one launch (start us, length us, event | category | flops | bytes accessed | tf_op | source)
XLA Modules:
  0.0 430.1 jit_solution(9382901780992876249)
XLA Ops:
  7.9 2.3 copy.20
  10.2 4.5 %all-to-all-start = ((bf16[512,8,128]{0,2,1:T(8,128)(2,1)}), bf16[512,8,128]{0,2,1:T(8,128)(2,1)S(1)}, u32[]{:S(2)}, u32[]{:S(2)}) async-start(bf16[512,8,128]{0,2,1:T(8,128)(2,1)} %bitcast), calls=%async_computation | async-start | bytes 2097152 | tf_op jit(solution)/shard_map/all_to_all | solution.py:90
  14.7 23.0 %gather_fusion = s32[4096]{0:T(1024)S(1)} fusion(s32[65536]{0:T(1024)S(1)} %copy-done, s32[4096]{0:T(1024)S(1)} %fusion.25), kind=kCustom, calls=%fused_computation | custom fusion | bytes 49152 | tf_op jit(solution)/shard_map/gather | solution.py:92
  37.8 23.0 %gather_fusion.1 = s32[4096]{0:T(1024)S(1)} fusion(s32[65536]{0:T(1024)S(1)} %copy-done.1, s32[4096]{0:T(1024)S(1)} %fusion.25), kind=kCustom, calls=%fused_computation.1 | custom fusion | bytes 49152 | tf_op jit(solution)/shard_map/gather | solution.py:93
  62.1 89.9 %all-gather.2.cloned.1.call-done = bf16[65536,128]{1,0:T(8,128)(2,1)} async-done(((bf16[2048,128]{1,0:T(8,128)(2,1)}), bf16[65536,128]{1,0:T(8,128)(2,1)}) %all-gather.2.cloned.1.call-update) | async-done | bytes 16777232 | tf_op jit(solution)/shard_map/all_gather | solution.py:94
  152.0 19.0 %gather_fusion.2 = bf16[4096,128]{1,0:T(8,128)(2,1)S(1)} fusion(bf16[65536,128]{1,0:T(8,128)(2,1)} %all-gather.2.cloned.1.call-done, s32[4096]{0:T(1024)S(1)} %broadcast_clamp_fusion), kind=kCustom, calls=%fused_computation.2 | custom fusion | bytes 2113536 | tf_op jit(solution)/shard_map/jit(_take)/gather | solution.py:95
  172.3 2.9 subtract_convert_fusion
  175.2 2.3 copy.23
  177.5 46.6 %while.26 = (s32[]{:T(128)}, f32[1,2048,128]{2,1,0:T(8,128)S(1)}, f32[1,2048]{1,0:T(1,128)S(1)}, bf16[8,512,1,128]{3,1,2,0:T(8,128)(2,1)}, bf16[1,2048,128]{2,1,...) while((s32[]{:T(128)}, f32[1,2048,128]{2,1,0:T(8,128)S(1)}, ...), condition=%wide.region_5.6_spmd.clone, body=%wide.region_1.5_spmd.clone.sunk | while | flops 548930560 | bytes 19713120 | solution.py:85
  181.3 1.9 fusion.47
  183.3 1.9 fusion.45
  187.1 1.9 fusion.47
  189.1 1.9 fusion.45
  193.0 1.9 fusion.47
  195.0 1.9 fusion.45
  198.8 1.9 fusion.47
  200.8 1.9 fusion.45
  204.6 1.9 fusion.47
  206.6 1.9 fusion.45
  210.5 1.9 fusion.47
  212.4 1.9 fusion.45
  216.3 1.9 fusion.47
  218.3 1.9 fusion.45
  222.1 1.9 fusion.47
  225.5 35.6 %all_to_all.43 = f32[32,1,8256]{2,1,0:T(1,128)S(1)} all-to-all(f32[32,1,8256]{2,1,0:T(1,128)S(1)} %all_to_all.32), channel_id=1, replica_groups=mesh['wide'=32,'narrow'=8] {'wide'}, dimensions={0} | all-to-all | bytes 2113536 | tf_op jit(solution)/shard_map/all_to_all | solution.py:21
  263.2 5.5 %all-to-all-start.2 = ((f32[32,1,8256]{2,1,0:T(1,128)}), f32[32,1,8256]{2,1,0:T(1,128)S(1)}, u32[]{:S(2)}, u32[]{:S(2)}) async-start(f32[32,1,8256]{2,1,0:T(1,128)} %broadcast_in_dim.41), calls=%async_computation.2 | async-start | bytes 2129920 | tf_op jit(solution)/shard_map/all_to_all | solution.py:32
  268.7 27.2 %all-to-all-done.2 = f32[32,1,8256]{2,1,0:T(1,128)S(1)} async-done(((f32[32,1,8256]{2,1,0:T(1,128)}), f32[32,1,8256]{2,1,0:T(1,128)S(1)}, u32[]{:S(2)}, u32[]{:S(2)}) %all-to-all-start.2) | async-done | bytes 1056800 | tf_op jit(solution)/shard_map/all_to_all | solution.py:32
  295.9 2.5 reduce.16
  299.7 2.2 multiply_reduce_fusion
  303.1 46.6 %while.27 = (s32[]{:T(128)}, f32[1,2048,128]{2,1,0:T(8,128)S(1)}, f32[1,2048]{1,0:T(1,128)S(1)}, bf16[8,512,1,128]{3,1,2,0:T(8,128)(2,1)}, bf16[1,2048,128]{2,1,...) while((s32[]{:T(128)}, f32[1,2048,128]{2,1,0:T(8,128)S(1)}, ...), condition=%wide.region_12.13_spmd.clone, body=%wide.region_8.12_spmd.clone.sunk | while | flops 548930560 | bytes 19713120 | solution.py:85
  306.9 2.0 fusion.53
  308.9 1.9 fusion.51
  312.7 1.9 fusion.53
  314.7 1.9 fusion.51
  318.6 1.9 fusion.53
  324.4 1.9 fusion.53
  330.2 1.9 fusion.53
  332.2 1.9 fusion.51
  336.0 1.9 fusion.53
  341.9 1.9 fusion.53
  343.9 1.9 fusion.51
  347.7 1.9 fusion.53
  351.1 33.2 %all_to_all.44 = f32[32,1,8256]{2,1,0:T(1,128)S(1)} all-to-all(f32[32,1,8256]{2,1,0:T(1,128)S(1)} %all_to_all.35), channel_id=1, replica_groups=mesh['wide'=32,'narrow'=8] {'wide'}, dimensions={0} | all-to-all | bytes 2113536 | tf_op jit(solution)/shard_map/all_to_all | solution.py:21
  386.4 5.7 %all-to-all-start.4 = ((f32[32,1,8256]{2,1,0:T(1,128)}), f32[32,1,8256]{2,1,0:T(1,128)}, u32[]{:S(2)}, u32[]{:S(2)}) async-start(f32[32,1,8256]{2,1,0:T(1,128)} %broadcast_in_dim.42), calls=%async_computation.4 | async-start | bytes 2129920 | tf_op jit(solution)/shard_map/all_to_all | solution.py:32
  393.8 2.0 copy.21
  395.8 2.9 fusion.20
  398.7 19.1 %all-to-all-done.4 = f32[32,1,8256]{2,1,0:T(1,128)} async-done(((f32[32,1,8256]{2,1,0:T(1,128)}), f32[32,1,8256]{2,1,0:T(1,128)}, u32[]{:S(2)}, u32[]{:S(2)}) %all-to-all-start.4) | async-done | bytes 1056800 | tf_op jit(solution)/shard_map/all_to_all | solution.py:32
  417.8 3.8 reduce.17
  (105 shorter events, 56.5 us)
Async XLA Ops:
  7.2 7.5 %copy-start = (s32[65536]{0:T(1024)S(1)}, s32[65536]{0:T(1024)}, u32[]{:S(2)}) copy-start(s32[65536]{0:T(1024)} %param.12) | copy-start | bytes 786436
  7.2 144.8 %all-gather.2.cloned.1.call-start = ((), (), s32[]{:S(2)}) async-start(), calls=%async_computation.5 | async-start | bytes 17301504 | tf_op jit(solution)/shard_map/all_gather | solution.py:94
  7.9 6.8 %copy-start.10 = (s32[4096]{0:T(1024)S(1)}, s32[4096]{0:T(1024)}, u32[]{:S(2)}) copy-start(s32[4096]{0:T(1024)} %param.14) | copy-start | bytes 49156
  10.2 162.1 %all-to-all-start = ((bf16[512,8,128]{0,2,1:T(8,128)(2,1)}), bf16[512,8,128]{0,2,1:T(8,128)(2,1)S(1)}, u32[]{:S(2)}, u32[]{:S(2)}) async-start(bf16[512,8,128]{0,2,1:T(8,128)(2,1)} %bitcast), calls=%async_computation | async-start | bytes 2097152 | tf_op jit(solution)/shard_map/all_to_all | solution.py:90
  14.7 23.1 %copy-start.1 = (s32[65536]{0:T(1024)S(1)}, s32[65536]{0:T(1024)}, u32[]{:S(2)}) copy-start(s32[65536]{0:T(1024)} %param.13) | copy-start | bytes 786436
  37.8 23.2 %copy-start.9 = (f32[1,2048,128]{2,1,0:T(8,128)S(1)}, f32[1,2048,128]{2,1,0:T(8,128)}, u32[]{:S(2)}) copy-start(f32[1,2048,128]{2,1,0:T(8,128)} %param.15) | copy-start | bytes 3145732
  170.9 4.3 copy-start.2
  172.3 5.2 %copy-start.6 = (bf16[512,8,128]{0,2,1:T(8,128)(2,1)}, bf16[512,8,128]{0,2,1:T(8,128)(2,1)S(1)}, u32[]{:S(2)}) copy-start(bf16[512,8,128]{0,2,1:T(8,128)(2,1)S(1)} %all-to-all-done) | copy-start | bytes 3145732
  263.2 32.6 %all-to-all-start.2 = ((f32[32,1,8256]{2,1,0:T(1,128)}), f32[32,1,8256]{2,1,0:T(1,128)S(1)}, u32[]{:S(2)}, u32[]{:S(2)}) async-start(f32[32,1,8256]{2,1,0:T(1,128)} %broadcast_in_dim.41), calls=%async_computation.2 | async-start | bytes 2129920 | tf_op jit(solution)/shard_map/all_to_all | solution.py:32
  298.7 1.0 copy-start.8
  301.9 1.2 copy-start.4
  384.2 7.9 %copy-start.7 = (bf16[512,8,128]{0,2,1:T(8,128)(2,1)S(1)}, bf16[512,8,128]{0,2,1:T(8,128)(2,1)}, u32[]{:S(2)}) copy-start(bf16[512,8,128]{0,2,1:T(8,128)(2,1)} %copy-done.6) | copy-start | bytes 3145732
  386.4 31.4 %all-to-all-start.4 = ((f32[32,1,8256]{2,1,0:T(1,128)}), f32[32,1,8256]{2,1,0:T(1,128)}, u32[]{:S(2)}, u32[]{:S(2)}) async-start(f32[32,1,8256]{2,1,0:T(1,128)} %broadcast_in_dim.42), calls=%async_computation.4 | async-start | bytes 2129920 | tf_op jit(solution)/shard_map/all_to_all | solution.py:32
  393.8 2.0 copy-start.3
  398.7 23.3 %copy-start.5 = (f32[1,2048,128]{2,1,0:T(8,128)S(1)}, f32[1,2048,128]{2,1,0:T(8,128)}, u32[]{:S(2)}) copy-start(f32[1,2048,128]{2,1,0:T(8,128)} %copy-done.4) | copy-start | bytes 3145732
Sparse Core Ops, SparseCore 0:
  10.6 141.3 all-gather.1
where the time goes:
time: 432 us; the launch traced here: 430 us
  waiting for transfers between devices  137 us (32%)
  local copies, waits for them, and re-layouts  80.5 us (19%)
  blocking collectives  68.8 us (16%)
  matrix products  61.8 us (14%)
  other arithmetic  51.6 us (12%)
  starting transfers between devices  15.7 us (4%)
  between operations  14.4 us (3%)
    all_gather x1, waiting for transfers between devices, on_device(): whole = lax.all_gather(centroid_table, 'wide', axis=0, tiled=True)  89.9 us
    all_to_all x2, blocking collectives, summed_on_arrival(): tiles = lax.all_to_all(cut_along(value, dim, count), axis, 0, 0, tiled=True)  68.8 us
    all_to_all x2, waiting for transfers between devices, from_everyone(): lax.all_to_all(jnp.broadcast_to(value[None], (count, *value.shape)), axis...  46.3 us
    dot_general x16, matrix products, block_step(): jnp.einsum('mbk,bms->mks', weights_soft, row_block, preferred_element_typ...  31.2 us
    dot_general x16, matrix products, block_step(): jnp.einsum('bms,mks->mbk', row_block, narrow_words, preferred_element_typ...  30.6 us
    gather x1, local copies, waits for them, and re-layouts, on_device(): owner_of = owner[assign]  23 us
    gather x1, local copies, waits for them, and re-layouts, on_device(): slot_of = slot[assign]  23 us
    gather x2, local copies, waits for them, and re-layouts, on_device(): jnp.take(whole, owner_of * centroid_table.shape[0] + slot_of, axis=0)  20.3 us
  transfers between devices with their start and end apart: 4, of which 3 were waited for; matrix products, arithmetic and copies ran while one was open for 18% of the time, Pallas kernels for 0%

commit v1 on v0

v1 whole, which is shorter than its diff:
```python
import functools
import math

import jax
import jax.numpy as jnp
from jax import lax
from jax.experimental import pallas as pl
from jax.experimental.pallas import tpu as pltpu
from jax.sharding import PartitionSpec as P

ITERS = 2
NZ, NX, NN = 8, 4, 8
NW = NZ * NX
CAP = 256
ROWS = 4096
K = 2048
SUB = 128
PART = 512
XK = K // NX
OWN = XK // NZ
BLK = 512
MESH = pl.DeviceIdType.MESH
f32, bf16, i32 = jnp.float32, jnp.bfloat16, jnp.int32


def iota(shape, dim):
    return lax.broadcasted_iota(i32, shape, dim)


def hot(mask):
    return jnp.where(mask, 1.0, 0.0).astype(bf16)


def nt(a, b):
    return lax.dot_general(a, b, (((1,), (1,)), ((), ())), preferred_element_type=f32)


def greet(peers):
    barrier = pltpu.get_barrier_semaphore()
    for peer in peers:
        pl.semaphore_signal(barrier, inc=1, device_id=peer, device_id_type=MESH)
    pl.semaphore_wait(barrier, len(peers))


def exchange_kernel(
    samples, table, lut, assign, out,
    samp, tabs, req, reqin, gs, gin, upper, codes, picked, centre,
    own_sem, s_send, s_recv, up_send, up_recv, dn_send, dn_recv,
    q_send, q_recv, g_send, g_recv,
):
    w = lax.axis_index("wide")
    n = lax.axis_index("narrow")
    z = w // NX
    x = lax.rem(w, NX)

    def at_zx(zz, xx):
        return {"wide": lax.rem(zz + NZ, NZ) * NX + lax.rem(xx + NX, NX)}

    xpeers = [at_zx(z, x + d) for d in range(1, NX)]
    npeers = [{"narrow": lax.rem(n + d, NN)} for d in range(1, NN)]
    above, below = at_zx(z + 1, x), at_zx(z - 1, x)
    greet([above, below] + xpeers + npeers)

    def copy(src, dst, send, recv, dev):
        return pltpu.make_async_remote_copy(
            src_ref=src, dst_ref=dst, send_sem=send, recv_sem=recv,
            device_id=dev, device_id_type=MESH,
        )

    def up(i):
        if i < 2:
            src, zo = table.at[i], z
        else:
            zo = lax.rem(z - i // 2 + NZ, NZ)
            src = tabs.at[zo, i % 2]
        return copy(src, tabs.at[zo, i % 2], up_send.at[i], up_recv.at[i], above)

    def half_of(i):
        return 1 if i == 6 else i % 2

    def down(i):
        if i < 2:
            src, zo = table.at[i], z
        else:
            zo = lax.rem(z + i // 2, NZ)
            src = tabs.at[zo, half_of(i)]
        return copy(src, tabs.at[zo, half_of(i)], dn_send.at[i], dn_recv.at[i], below)

    for i in range(2):
        up(i).start()
        down(i).start()

    own_tab = pltpu.make_async_copy(table, tabs.at[z], own_sem.at[0])
    own_tab.start()
    mine = pl.ds(pl.multiple_of(n * SUB, SUB), SUB)
    here = pl.ds(pl.multiple_of(n * PART, PART), PART)
    own_samp = pltpu.make_async_copy(samples.at[:, mine], samp.at[here], own_sem.at[1])
    own_samp.start()
    s_copies = []
    for d in range(1, NN):
        there = pl.ds(pl.multiple_of(lax.rem(n + d, NN) * SUB, SUB), SUB)
        c = copy(samples.at[:, there], samp.at[here], s_send.at[d - 1], s_recv.at[d - 1], npeers[d - 1])
        c.start()
        s_copies.append(c)

    upper[...] = hot(iota((BLK, BLK), 0) < iota((BLK, BLK), 1))
    picked[...] = jnp.zeros_like(picked)
    centre[...] = jnp.zeros_like(centre)

    def prep(b, carry):
        cols = pl.ds(pl.multiple_of(b * BLK, BLK), BLK)
        a = assign[:, cols]
        near = hot(iota((512, BLK), 0) == (a >> 7))
        found = jnp.dot(lut[...], near, preferred_element_type=f32)
        sel = iota((128, BLK), 0) == (a & 127)
        high = jnp.sum(jnp.where(sel, found[:128], 0.0), axis=0, keepdims=True)
        low = jnp.sum(jnp.where(sel, found[128:], 0.0), axis=0, keepdims=True)
        pos = (high * 256.0 + low).astype(i32)
        owner = pos >> 11
        slot = pos & 2047
        order = (owner & 3) * NZ + (owner >> 2)
        member = jnp.where(iota((NW, BLK), 0) == order, 1.0, 0.0)
        before = jnp.dot(member.astype(bf16), upper[...], preferred_element_type=f32) + carry
        rank = jnp.sum(member * before, axis=0, keepdims=True).astype(i32)
        codes[:, cols] = owner * CAP + rank
        parts = jnp.concatenate(
            [member * (slot >> 8).astype(f32), member * (slot & 255).astype(f32)], axis=0
        ).astype(bf16)
        picked[...] += nt(parts, hot(iota((CAP, BLK), 0) == rank))
        return carry + jnp.sum(member, axis=1, keepdims=True)

    lax.fori_loop(0, ROWS // BLK, prep, jnp.zeros((NW, 1), f32))
    slots = (picked[:NW] * 256.0 + picked[NW:]).astype(i32)
    for d in range(NX):
        req[d] = slots[d * NZ : (d + 1) * NZ]
    q_copies = []
    for d in range(1, NX):
        xx = lax.rem(x + d, NX)
        c = copy(req.at[xx], reqin.at[x], q_send.at[d - 1], q_recv.at[d - 1], xpeers[d - 1])
        c.start()
        q_copies.append(c)
    reqin[x] = req[x]
    own_tab.wait()
    for c in q_copies:
        c.wait()

    def give(j, d):
        return copy(
            gs.at[j, d - 1], gin.at[j, x], g_send.at[j, d - 1], g_recv.at[j, d - 1],
            {"wide": z * NX + lax.rem(x + d, NX)},
        )

    def table_of(j):
        step = (j + 1) // 2
        return lax.rem(z + step * (1 - 2 * lax.rem(j, 2)) + NZ, NZ)

    def gather(j):
        zo = table_of(j)

        def rows_for(d):
            xx = lax.rem(x + d, NX)
            want = reqin[xx, pl.ds(zo, 1), :]
            got = jnp.zeros((SUB, CAP), f32)
            for h in range(2):
                pick = hot(iota((K // 2, CAP), 0) + h * (K // 2) == want)
                got = got + jnp.dot(tabs[zo, h], pick, preferred_element_type=f32)
            return got.astype(bf16)

        def one(d, _):
            gs[j, d - 1] = rows_for(d)
            give(j, d).start()
            return 0

        lax.fori_loop(1, NX, one, 0)
        gin[j, x] = rows_for(0)

    def consume(j):
        zo = table_of(j)

        def arrived(d, _):
            give(j, d).wait_recv()
            return 0

        lax.fori_loop(1, NX, arrived, 0)
        rows = jnp.concatenate([gin[j, d] for d in range(NX)], axis=1)

        def place(b, _):
            cols = pl.ds(pl.multiple_of(b * BLK, BLK), BLK)
            where = codes[:, cols] - zo * (NX * CAP)
            spot = hot(iota((NX * CAP, BLK), 0) == where)
            centre[:, cols] += jnp.dot(rows, spot, preferred_element_type=f32)
            return 0

        lax.fori_loop(0, ROWS // BLK, place, 0)

    due = {1: (0, 1), 2: (2,), 3: (3,), 4: (4,), 5: (5,), 7: (6,)}

    def forward(i):
        up(i).wait_recv()
        if i + 2 <= 6:
            up(i + 2).start()
        down(i).wait_recv()
        if i == 5:
            down(6).start()
        elif i + 2 <= 5:
            down(i + 2).start()

    def step(j, _):
        for when, which in due.items():
            @pl.when(j == when)
            def _():
                for i in which:
                    forward(i)

        gather(j)

        @pl.when(j > 0)
        def _():
            consume(j - 1)

        return 0

    lax.fori_loop(0, NZ, step, 0)
    consume(NZ - 1)
    own_samp.wait()
    for c in s_copies:
        c.wait()

    def finish(b, _):
        at = pl.ds(pl.multiple_of(b * BLK, BLK), BLK)
        mid = centre[:, at].T
        out[at, :] = (samp[at, :].astype(f32) - mid).astype(bf16)
        return 0

    lax.fori_loop(0, ROWS // BLK, finish, 0)
    for i in range(7):
        up(i).wait_send()
        down(i).wait_send()

    def sent(k, _):
        give(k // 3, lax.rem(k, 3) + 1).wait_send()
        return 0

    lax.fori_loop(0, NZ * 3, sent, 0)


RB = 256
SCALE = math.log2(math.e) / 8.0


def em_kernel(
    rows, book, out,
    aug, scaled, words, probs, score,
    xs, xc, xin, xcin, zs, zc, zin, zcin, fresh, norm, normz, normx, own,
    x_send, x_recv, xc_send, xc_recv, z_send, z_recv, zc_send, zc_recv,
    az_send, az_recv, an_send, an_recv, ax_send, ax_recv, am_send, am_recv,
):
    w = lax.axis_index("wide")
    z = w // NX
    x = lax.rem(w, NX)
    xpeers = [{"wide": z * NX + lax.rem(x + d, NX)} for d in range(1, NX)]
    zpeers = [{"wide": lax.rem(z + d, NZ) * NX + x} for d in range(1, NZ)]
    greet(xpeers + zpeers)

    def copy(src, dst, send, recv, dev):
        return pltpu.make_async_remote_copy(
            src_ref=src, dst_ref=dst, send_sem=send, recv_sem=recv,
            device_id=dev, device_id_type=MESH,
        )

    lane = iota((1, SUB), 1)

    def extra(half):
        hi = half.astype(bf16).astype(f32)
        mid = (half - hi).astype(bf16).astype(f32)
        lo = half - hi - mid
        return jnp.where(lane == 0, hi, jnp.where(lane == 1, mid, jnp.where(lane == 2, lo, 0.0)))

    aug[:, :SUB] = rows[...]
    aug[:, SUB:] = jnp.broadcast_to(jnp.where(lane < 3, 1.0, 0.0), (ROWS, SUB)).astype(bf16)

    def load(b, _):
        at = pl.ds(pl.multiple_of(b * 256, 256), 256)
        c = book[at, :]
        words[at, :SUB] = c.astype(bf16)
        words[at, SUB:] = extra(-0.5 * jnp.sum(c * c, axis=1, keepdims=True)).astype(bf16)
        return 0

    lax.fori_loop(0, K // 256, load, 0)
    base = pl.multiple_of(x * XK, XK)
    first = pl.multiple_of(base + z * OWN, OWN)
    own[...] = book[pl.ds(first, OWN), :]
    pending = []

    for it in range(ITERS):
        def block(b, _):
            at = pl.ds(pl.multiple_of(b * RB, RB), RB)
            r = aug[at, :]
            score[...] = nt(words[...], r)
            top = jnp.max(score[...], axis=0, keepdims=True)
            p = jnp.exp2((score[...] - top) * SCALE)
            probs[:, at] = p.astype(bf16)
            inv = 1.0 / jnp.sum(p, axis=0, keepdims=True)
            invt = jnp.broadcast_to(inv, (SUB, RB)).T
            scaled[at, :SUB] = (r[:, :SUB].astype(f32) * invt).astype(bf16)
            hi = invt.astype(bf16).astype(f32)
            scaled[at, SUB:] = jnp.where(lane == 0, hi, jnp.where(lane == 1, invt - hi, 0.0)).astype(bf16)
            return 0

        lax.fori_loop(0, ROWS // RB, block, 0)

        def chunk(xx):
            at = pl.ds(pl.multiple_of(xx * XK, XK), XK)
            t = jnp.dot(probs[at, :], scaled[...], preferred_element_type=f32)
            c = t[:, SUB : SUB + 1] + t[:, SUB + 1 : SUB + 2]
            spread = jnp.where(iota((XK, SUB), 1) == lax.rem(iota((XK, SUB), 0), SUB), c, 0.0)
            c = jnp.sum(spread.reshape(XK // SUB, SUB, SUB), axis=1)
            return t[:, :SUB], jnp.concatenate([c, jnp.zeros_like(c)], axis=0)

        sends = []
        for d in (2, 1, 3):
            t, c = chunk(lax.rem(x + d, NX))
            xs[it, d - 1] = t.astype(bf16)
            xc[it, d - 1] = c
            a = copy(xs.at[it, d - 1], xin.at[it, d - 1], x_send.at[it, d - 1], x_recv.at[it, d - 1], xpeers[d - 1])
            e = copy(xc.at[it, d - 1], xcin.at[it, d - 1], xc_send.at[it, d - 1], xc_recv.at[it, d - 1], xpeers[d - 1])
            a.start()
            e.start()
            sends += [a, e]
        total, count = chunk(x)
        for s in sends:
            s.wait_recv()
        for d in range(3):
            total = total + xin[it, d].astype(f32)
            count = count + xcin[it, d]
        zs[it] = total.astype(bf16)
        score[pl.ds(0, XK), :SUB] = total
        zc[it] = count
        pending += sends

        sends = []
        for d in (4, 3, 5, 2, 6, 1, 7):
            zz = lax.rem(z + d, NZ)
            a = copy(zs.at[it, pl.ds(pl.multiple_of(zz * OWN, OWN), OWN)], zin.at[it, d - 1],
                     z_send.at[it, d - 1], z_recv.at[it, d - 1], zpeers[d - 1])
            e = copy(zc.at[it], zcin.at[it, d - 1], zc_send.at[it, d - 1], zc_recv.at[it, d - 1], zpeers[d - 1])
            a.start()
            e.start()
            sends += [a, e]
        part = score[pl.ds(pl.multiple_of(z * OWN, OWN), OWN), :SUB]
        for s in sends:
            s.wait_recv()
        for d in range(NZ - 1):
            part = part + zin[it, d].astype(f32)
            count = count + zcin[it, d]
        pending += sends
        normz[...] = count
        line = normz[pl.ds(z // 2, 1), :]
        spot = iota((OWN, SUB), 1) == iota((OWN, SUB), 0) + lax.rem(z, 2) * OWN
        cnt = jnp.sum(jnp.where(spot, jnp.broadcast_to(line, (OWN, SUB)), 0.0), axis=1, keepdims=True)
        new = (part + own[...]) / (cnt + 1.0)
        own[...] = new
        fresh[it, pl.ds(first, OWN), :] = new.astype(bf16)
        last = it == ITERS - 1
        if not last:
            half = -0.5 * jnp.sum(new * new, axis=1, keepdims=True)
            flat = jnp.sum(jnp.where(spot, half, 0.0), axis=0, keepdims=True)
            norm[...] = jnp.where(iota((8, SUB), 0) == z // 2, flat, 0.0)

        sends = []
        for d in (4, 3, 5, 2, 6, 1, 7):
            src = fresh.at[it, pl.ds(first, OWN)]
            a = copy(src, src, az_send.at[it, d - 1], az_recv.at[it, d - 1], zpeers[d - 1])
            a.start()
            sends.append(a)
            if not last:
                e = copy(norm, normx.at[NX + d - 1], an_send.at[d - 1], an_recv.at[d - 1], zpeers[d - 1])
                e.start()
                sends.append(e)
        for s in sends:
            s.wait_recv()
        pending += sends
        if not last:
            mine = norm[...]
            for d in range(NZ - 1):
                mine = mine + normx[NX + d]
            normx[x] = mine
        sends = []
        for d in (2, 1, 3):
            src = fresh.at[it, pl.ds(base, XK)]
            a = copy(src, src, ax_send.at[it, d - 1], ax_recv.at[it, d - 1], xpeers[d - 1])
            a.start()
            sends.append(a)
            if not last:
                e = copy(normx.at[x], normx.at[x], am_send.at[d - 1], am_recv.at[d - 1], xpeers[d - 1])
                e.start()
                sends.append(e)
        for s in sends:
            s.wait_recv()
        pending += sends
        if last:
            out[...] = fresh[it].astype(f32)
        else:
            words[:, :SUB] = fresh[it]
            for xx in range(NX):
                for q in range(XK // SUB):
                    at = pl.ds(xx * XK + q * SUB, SUB)
                    half = jnp.broadcast_to(normx[xx, q : q + 1, :], (SUB, SUB)).T
                    words[at, SUB:] = extra(half).astype(bf16)
    for s in pending:
        s.wait_send()


def vmem():
    return pl.BlockSpec(memory_space=pltpu.VMEM)


def exchange(samples, table, lut, assign):
    dma = pltpu.SemaphoreType.DMA
    return pl.pallas_call(
        exchange_kernel,
        out_shape=jax.ShapeDtypeStruct((ROWS, SUB), bf16),
        in_specs=[pl.BlockSpec(memory_space=pl.ANY), vmem(), vmem(), vmem()],
        out_specs=vmem(),
        scratch_shapes=[
            pltpu.VMEM((ROWS, SUB), bf16),
            pltpu.VMEM((NZ, 2, SUB, K // 2), bf16),
            pltpu.VMEM((NX, NZ, CAP), i32),
            pltpu.VMEM((NX, NZ, CAP), i32),
            pltpu.VMEM((NZ, NX - 1, SUB, CAP), bf16),
            pltpu.VMEM((NZ, NX, SUB, CAP), bf16),
            pltpu.VMEM((BLK, BLK), bf16),
            pltpu.VMEM((1, ROWS), i32),
            pltpu.VMEM((2 * NW, CAP), f32),
            pltpu.VMEM((SUB, ROWS), f32),
            dma((2,)), dma((7,)), dma((7,)), dma((7,)), dma((7,)), dma((7,)), dma((7,)),
            dma((3,)), dma((3,)), dma((NZ, 3)), dma((NZ, 3)),
        ],
        compiler_params=pltpu.CompilerParams(
            collective_id=0, has_side_effects=True, vmem_limit_bytes=48 << 20
        ),
        name="exchange",
    )(samples, table, lut, assign)


def refine(rows, book):
    dma = pltpu.SemaphoreType.DMA
    x3, z7 = (ITERS, 3), (ITERS, 7)
    return pl.pallas_call(
        em_kernel,
        out_shape=jax.ShapeDtypeStruct((K, SUB), f32),
        in_specs=[vmem(), vmem()],
        out_specs=vmem(),
        scratch_shapes=[
            pltpu.VMEM((ROWS, 2 * SUB), bf16),
            pltpu.VMEM((ROWS, 2 * SUB), bf16),
            pltpu.VMEM((K, 2 * SUB), bf16),
            pltpu.VMEM((K, ROWS), bf16),
            pltpu.VMEM((K, RB), f32),
            pltpu.VMEM((ITERS, 3, XK, SUB), bf16),
            pltpu.VMEM((ITERS, 3, 8, SUB), f32),
            pltpu.VMEM((ITERS, 3, XK, SUB), bf16),
            pltpu.VMEM((ITERS, 3, 8, SUB), f32),
            pltpu.VMEM((ITERS, XK, SUB), bf16),
            pltpu.VMEM((ITERS, 8, SUB), f32),
            pltpu.VMEM((ITERS, 7, OWN, SUB), bf16),
            pltpu.VMEM((ITERS, 7, 8, SUB), f32),
            pltpu.VMEM((ITERS, K, SUB), bf16),
            pltpu.VMEM((8, SUB), f32),
            pltpu.VMEM((8, SUB), f32),
            pltpu.VMEM((NX + 7, 8, SUB), f32),
            pltpu.VMEM((OWN, SUB), f32),
            dma(x3), dma(x3), dma(x3), dma(x3), dma(z7), dma(z7), dma(z7), dma(z7),
            dma(z7), dma(z7), dma((7,)), dma((7,)), dma(x3), dma(x3), dma((3,)), dma((3,)),
        ],
        compiler_params=pltpu.CompilerParams(
            collective_id=1, has_side_effects=True, vmem_limit_bytes=56 << 20
        ),
        name="refine",
    )(rows, book)


def on_device(samples, centroid_table, owner, slot, assign, codebook):
    pos = (owner * K + slot).reshape(512, 128)
    lut = jnp.concatenate([(pos >> 8).T, (pos & 255).T], axis=0).astype(bf16)
    table = centroid_table.reshape(2, K // 2, SUB).transpose(0, 2, 1)
    residual = exchange(samples, table, lut, assign.reshape(1, ROWS))
    refined = refine(residual, codebook[0])
    return residual, refined[None]


def solution(mesh):
    return jax.shard_map(
        on_device,
        mesh=mesh,
        in_specs=(
            P(("wide", "narrow"), None),
            P("wide", "narrow"),
            P(),
            P(),
            P("wide"),
            P("narrow", None, None),
        ),
        out_specs=(P("wide", "narrow"), P("narrow", None, None)),
        check_vma=False,
    )
```

time: 432 us -> 179 us (0.41)
  Pallas kernels: 0 us -> 170 us
  waiting for transfers between devices: 137 us -> 0 us
  local copies, waits for them, and re-layouts: 80.5 us -> 6.07 us
  blocking collectives: 68.8 us -> 0 us
  matrix products: 61.8 us -> 0 us
  other arithmetic: 51.6 us -> 1.12 us
  starting transfers between devices: 15.7 us -> 0 us
  between operations: 14.4 us -> 0.71 us
    pallas_call x0 -> x2, Pallas kernels: none -> 170 us  [the longest x1 107 us: refine(): pl.pallas_call(em_kernel, out_shape=jax.ShapeDtypeStruct((K, SUB), f32),...]
    all_gather x1 -> x0, waiting for transfers between devices: 89.9 us -> none  [on_device(): whole = lax.all_gather(centroid_table, 'wide', axis=0, tiled=True)]
    all_to_all x2 -> x0, blocking collectives: 68.8 us -> none  [summed_on_arrival(): tiles = lax.all_to_all(cut_along(value, dim, count), axis, 0, 0, tiled=True)]
    gather x4 -> x0, local copies, waits for them, and re-layouts: 66.4 us -> none  [the longest x1 23 us: on_device(): owner_of = owner[assign]]
    dot_general x32 -> x0, matrix products: 61.8 us -> none  [the longest x16 31.2 us: block_step(): jnp.einsum('mbk,bms->mks', weights_soft, row_block, preferred_element_typ...]
    all_to_all x3 -> x0, waiting for transfers between devices: 46.3 us -> none  [the longest x2 46.3 us: from_everyone(): lax.all_to_all(jnp.broadcast_to(value[None], (count, *value.shape)), axis...]
    reduce_sum x36 -> x0, other arithmetic: 35 us -> none  [the longest x16 19.2 us: block_step(): jnp.sum(weights_soft, axis=1, dtype=jnp.float32)]
    all_to_all x3 -> x0, starting transfers between devices: 15.6 us -> none  [the longest x2 11.2 us: from_everyone(): lax.all_to_all(jnp.broadcast_to(value[None], (count, *value.shape)), axis...]
  transfers between devices with their start and end apart: 4 -> 0, of which waited for: 3 -> 0; matrix products, arithmetic and copies ran while one was open for 18% -> 0% of each run, Pallas kernels for 0% -> 0%
where the time goes in v1:
time: 179 us; the launch traced here: 178 us
  Pallas kernels  170 us (95%)
  local copies, waits for them, and re-layouts  6.07 us (3%)
    pallas_call x1, Pallas kernels, refine(): pl.pallas_call(em_kernel, out_shape=jax.ShapeDtypeStruct((K, SUB), f32),...  107 us
    pallas_call x1, Pallas kernels, exchange(): pl.pallas_call(exchange_kernel, out_shape=jax.ShapeDtypeStruct((ROWS, SUB...  63 us
    unnamed x12, local copies, waits for them, and re-layouts  5.63 us

profile of v1, /device:TPU:2, one launch (start us, length us, event | category | flops | bytes accessed | tf_op | source)
XLA Modules:
  0.0 177.7 jit_solution(10354577118512970691)
XLA Ops:
  0.6 1.1 fusion
  1.7 0.0 copy-start.4
  1.7 0.0 copy-start.1
  1.8 0.1 copy.9
  1.9 0.1 copy.10
  2.0 0.8 copy-done.4
  2.8 0.0 copy-start.2
  2.8 0.2 copy.8
  3.0 0.1 copy-done.1
  3.1 0.4 copy-done.2
  3.6 63.0 %exchange.1.rows = bf16[4096,128]{1,0:T(8,128)(2,1)S(1)} custom-call(bf16[512,1024]{1,0:T(8,128)(2,1)S(1)} %copy-done.1, bf16[2,128,1024]{2,1,0:T(8,128)(2,1)S(1)} %bitcast.11, bf16[256,512]{1,0:T(8,128)(2,1)S(1)} %pad_maximum_fusion.lut, s32[1,4096]{1,0:T(1,128)S(1)} %bitcast.12), custom_call_target="tpu_custom_call" | custom-call | tf_op jit(solution)/shard_map/exchange/pallas_call | solution.py:420
  66.6 0.0 copy-start
  66.6 1.0 copy-done
  67.6 106.8 %refine.1 = f32[2048,128]{1,0:T(8,128)} custom-call(bf16[4096,128]{1,0:T(8,128)(2,1)} %copy-done, f32[2048,128]{1,0:T(8,128)} %bitcast.14), custom_call_target="tpu_custom_call" | custom-call | tf_op jit(solution)/shard_map/refine/pallas_call | solution.py:449
  174.4 0.0 copy-start.3
  174.4 2.4 %copy.13 = bf16[4096,128]{1,0:T(8,128)(2,1)} copy(bf16[4096,128]{1,0:T(8,128)(2,1)} %copy-done) | data formatting | bytes 2097152
  176.7 0.0 copy-done.3
  176.7 1.0 copy.14
  (1 shorter events, 0.0 us)
Async XLA Ops:
  1.7 1.0 copy-start.4
  1.7 1.4 copy-start.1
  2.8 0.8 copy-start.2
  66.6 1.0 copy-start
  174.4 2.4 %copy-start.3 = (f32[2048,128]{1,0:T(8,128)S(1)}, f32[2048,128]{1,0:T(8,128)}, u32[]{:S(2)}) copy-start(f32[2048,128]{1,0:T(8,128)} %refine.1) | copy-start | bytes 3145732

commit v2 on v1

--- a/solution.py
+++ b/solution.py
@@ -166,15 +166,16 @@
                 got = got + jnp.dot(tabs[zo, h], pick, preferred_element_type=f32)
             return got.astype(bf16)
 
-        def one(d, _):
+        def one(e, _):
+            d = lax.rem(e + 1, NX - 1) + 1
             gs[j, d - 1] = rows_for(d)
             give(j, d).start()
             return 0
 
-        lax.fori_loop(1, NX, one, 0)
+        lax.fori_loop(0, NX - 1, one, 0)
         gin[j, x] = rows_for(0)
 
-    def consume(j):
+    def consume(j, last=False):
         zo = table_of(j)
 
         def arrived(d, _):
@@ -188,7 +189,11 @@
             cols = pl.ds(pl.multiple_of(b * BLK, BLK), BLK)
             where = codes[:, cols] - zo * (NX * CAP)
             spot = hot(iota((NX * CAP, BLK), 0) == where)
-            centre[:, cols] += jnp.dot(rows, spot, preferred_element_type=f32)
+            mid = centre[:, cols] + jnp.dot(rows, spot, preferred_element_type=f32)
+            if last:
+                out[cols, :] = (samp[cols, :].astype(f32) - mid.T).astype(bf16)
+            else:
+                centre[:, cols] = mid
             return 0
 
         lax.fori_loop(0, ROWS // BLK, place, 0)
@@ -214,25 +219,23 @@
 
         gather(j)
 
+        @pl.when(j == NZ - 1)
+        def _():
+            consume(NZ - 3)
+
         @pl.when(j > 0)
         def _():
-            consume(j - 1)
+            @pl.when(j != NZ - 2)
+            def _():
+                consume(j - 1)
 
         return 0
 
     lax.fori_loop(0, NZ, step, 0)
-    consume(NZ - 1)
     own_samp.wait()
     for c in s_copies:
         c.wait()
-
-    def finish(b, _):
-        at = pl.ds(pl.multiple_of(b * BLK, BLK), BLK)
-        mid = centre[:, at].T
-        out[at, :] = (samp[at, :].astype(f32) - mid).astype(bf16)
-        return 0
-
-    lax.fori_loop(0, ROWS // BLK, finish, 0)
+    consume(NZ - 1, last=True)
     for i in range(7):
         up(i).wait_send()
         down(i).wait_send()
@@ -244,14 +247,16 @@
     lax.fori_loop(0, NZ * 3, sent, 0)
 
 
-RB = 256
+RB = 512
+KC = 256
+XH = XK // 2
 SCALE = math.log2(math.e) / 8.0
 
 
 def em_kernel(
     rows, book, out,
-    aug, scaled, words, probs, score,
-    xs, xc, xin, xcin, zs, zc, zin, zcin, fresh, norm, normz, normx, own,
+    aug, scaled, words, probs, score, score2,
+    xs, keep, xc, xin, xcin, zs, zc, zin, zcin, fresh, norm, normz, normx, own,
     x_send, x_recv, xc_send, xc_recv, z_send, z_recv, zc_send, zc_recv,
     az_send, az_recv, an_send, an_recv, ax_send, ax_recv, am_send, am_recv,
 ):
@@ -293,21 +298,43 @@
     pending = []
 
     for it in range(ITERS):
-        def block(b, _):
-            at = pl.ds(pl.multiple_of(b * RB, RB), RB)
+        def rows_at(b):
+            return pl.ds(pl.multiple_of(b * RB, RB), RB)
+
+        def products(k, r, dst, top):
+            s = nt(words[k : k + KC, :], r)
+            dst[k : k + KC, :] = s
+            m = jnp.max(s.reshape(KC // 8, 8, RB), axis=0)
+            return m if top is None else jnp.maximum(top, m)
+
+        def both(nxt, dst, now, src, top):
+            ahead = aug[rows_at(nxt), :]
+            at = rows_at(now)
             r = aug[at, :]
-            score[...] = nt(words[...], r)
-            top = jnp.max(score[...], axis=0, keepdims=True)
-            p = jnp.exp2((score[...] - top) * SCALE)
-            probs[:, at] = p.astype(bf16)
-            inv = 1.0 / jnp.sum(p, axis=0, keepdims=True)
+            shift = jnp.max(top, axis=0, keepdims=True)
+            best, mass = None, jnp.zeros((8, RB), f32)
+            for k in range(0, K, KC):
+                best = products(k, ahead, dst, best)
+                p = jnp.exp2((src[k : k + KC, :] - shift) * SCALE)
+                probs[k : k + KC, at] = p.astype(bf16)
+                mass = mass + jnp.sum(p.reshape(KC // 8, 8, RB), axis=0)
+            inv = 1.0 / jnp.sum(mass, axis=0, keepdims=True)
             invt = jnp.broadcast_to(inv, (SUB, RB)).T
             scaled[at, :SUB] = (r[:, :SUB].astype(f32) * invt).astype(bf16)
             hi = invt.astype(bf16).astype(f32)
             scaled[at, SUB:] = jnp.where(lane == 0, hi, jnp.where(lane == 1, invt - hi, 0.0)).astype(bf16)
-            return 0
-
-        lax.fori_loop(0, ROWS // RB, block, 0)
+            return best
+
+        top = None
+        lead = aug[pl.ds(0, RB), :]
+        for k in range(0, K, KC):
+            top = products(k, lead, score, top)
+
+        def pair(i, top):
+            top = both(2 * i + 1, score2, 2 * i, score, top)
+            return both(lax.rem(2 * i + 2, ROWS // RB), score, 2 * i + 1, score2, top)
+
+        lax.fori_loop(0, ROWS // RB // 2, pair, top)
 
         def chunk(xx):
             at = pl.ds(pl.multiple_of(xx * XK, XK), XK)
@@ -317,22 +344,41 @@
             c = jnp.sum(spread.reshape(XK // SUB, SUB, SUB), axis=1)
             return t[:, :SUB], jnp.concatenate([c, jnp.zeros_like(c)], axis=0)
 
-        sends = []
-        for d in (2, 1, 3):
-            t, c = chunk(lax.rem(x + d, NX))
-            xs[it, d - 1] = t.astype(bf16)
+        right, across, left = xpeers
+
+        def tell(d, c):
             xc[it, d - 1] = c
-            a = copy(xs.at[it, d - 1], xin.at[it, d - 1], x_send.at[it, d - 1], x_recv.at[it, d - 1], xpeers[d - 1])
             e = copy(xc.at[it, d - 1], xcin.at[it, d - 1], xc_send.at[it, d - 1], xc_recv.at[it, d - 1], xpeers[d - 1])
+            e.start()
+            return e
+
+        def part_to(q, value, dev):
+            xs[it, q] = value.astype(bf16)
+            a = copy(xs.at[it, q], xin.at[it, q], x_send.at[it, q], x_recv.at[it, q], dev)
             a.start()
-            e.start()
-            sends += [a, e]
+            return a
+
+        t, c = chunk(lax.rem(x + 2, NX))
+        sends = [part_to(0, t[:XH], right), part_to(1, t[XH:], left), tell(2, c)]
+        t, c = chunk(lax.rem(x + 1, NX))
+        sends += [part_to(2, t[XH:], right), tell(1, c)]
+        keep[:XH] = t[:XH]
+        t, c = chunk(lax.rem(x + 3, NX))
+        sends += [part_to(3, t[:XH], left), tell(3, c)]
+        keep[XH:] = t[XH:]
+        sends[0].wait_recv()
+        relay = [part_to(4, keep[:XH] + xin[it, 0].astype(f32), right)]
+        sends[1].wait_recv()
+        relay.append(part_to(5, keep[XH:] + xin[it, 1].astype(f32), left))
         total, count = chunk(x)
-        for s in sends:
+        for s in sends[2:] + relay:
             s.wait_recv()
+        total = total + jnp.concatenate(
+            [xin[it, 4].astype(f32) + xin[it, 3].astype(f32),
+             xin[it, 5].astype(f32) + xin[it, 2].astype(f32)], axis=0)
         for d in range(3):
-            total = total + xin[it, d].astype(f32)
             count = count + xcin[it, d]
+        sends += relay
         zs[it] = total.astype(bf16)
         score[pl.ds(0, XK), :SUB] = total
         zc[it] = count
@@ -385,21 +431,29 @@
             for d in range(NZ - 1):
                 mine = mine + normx[NX + d]
             normx[x] = mine
-        sends = []
-        for d in (2, 1, 3):
-            src = fresh.at[it, pl.ds(base, XK)]
-            a = copy(src, src, ax_send.at[it, d - 1], ax_recv.at[it, d - 1], xpeers[d - 1])
+        def spread(q, xx, h, dev):
+            src = fresh.at[it, pl.ds(pl.multiple_of(xx * XK + h * XH, XH), XH)]
+            a = copy(src, src, ax_send.at[it, q], ax_recv.at[it, q], dev)
             a.start()
-            sends.append(a)
-            if not last:
+            return a
+
+        sends = [spread(0, x, 0, right), spread(1, x, 1, left)]
+        if not last:
+            for d in (2, 1, 3):
                 e = copy(normx.at[x], normx.at[x], am_send.at[d - 1], am_recv.at[d - 1], xpeers[d - 1])
                 e.start()
                 sends.append(e)
-        for s in sends:
+        sends += [spread(2, x, 1, right), spread(3, x, 0, left)]
+        sends[0].wait_recv()
+        relay = [spread(4, lax.rem(x + 3, NX), 0, right)]
+        sends[1].wait_recv()
+        relay.append(spread(5, lax.rem(x + 1, NX), 1, left))
+        sends = sends + relay
+        for s in sends[2:]:
             s.wait_recv()
         pending += sends
         if last:
-            out[...] = fresh[it].astype(f32)
+            out[...] = fresh[it]
         else:
             words[:, :SUB] = fresh[it]
             for xx in range(NX):
@@ -445,10 +499,10 @@
 
 def refine(rows, book):
     dma = pltpu.SemaphoreType.DMA
-    x3, z7 = (ITERS, 3), (ITERS, 7)
+    x3, z7, x6 = (ITERS, 3), (ITERS, 7), (ITERS, 6)
     return pl.pallas_call(
         em_kernel,
-        out_shape=jax.ShapeDtypeStruct((K, SUB), f32),
+        out_shape=jax.ShapeDtypeStruct((K, SUB), bf16),
         in_specs=[vmem(), vmem()],
         out_specs=vmem(),
         scratch_shapes=[
@@ -457,9 +511,11 @@
             pltpu.VMEM((K, 2 * SUB), bf16),
             pltpu.VMEM((K, ROWS), bf16),
             pltpu.VMEM((K, RB), f32),
-            pltpu.VMEM((ITERS, 3, XK, SUB), bf16),
+            pltpu.VMEM((K, RB), f32),
+            pltpu.VMEM((ITERS, 6, XH, SUB), bf16),
+            pltpu.VMEM((XK, SUB), f32),
             pltpu.VMEM((ITERS, 3, 8, SUB), f32),
-            pltpu.VMEM((ITERS, 3, XK, SUB), bf16),
+            pltpu.VMEM((ITERS, 6, XH, SUB), bf16),
             pltpu.VMEM((ITERS, 3, 8, SUB), f32),
             pltpu.VMEM((ITERS, XK, SUB), bf16),
             pltpu.VMEM((ITERS, 8, SUB), f32),
@@ -470,8 +526,8 @@
             pltpu.VMEM((8, SUB), f32),
             pltpu.VMEM((NX + 7, 8, SUB), f32),
             pltpu.VMEM((OWN, SUB), f32),
-            dma(x3), dma(x3), dma(x3), dma(x3), dma(z7), dma(z7), dma(z7), dma(z7),
-            dma(z7), dma(z7), dma((7,)), dma((7,)), dma(x3), dma(x3), dma((3,)), dma((3,)),
+            dma(x6), dma(x6), dma(x3), dma(x3), dma(z7), dma(z7), dma(z7), dma(z7),
+            dma(z7), dma(z7), dma((7,)), dma((7,)), dma(x6), dma(x6), dma((3,)), dma((3,)),
         ],
         compiler_params=pltpu.CompilerParams(
             collective_id=1, has_side_effects=True, vmem_limit_bytes=56 << 20
@@ -486,7 +542,7 @@
     table = centroid_table.reshape(2, K // 2, SUB).transpose(0, 2, 1)
     residual = exchange(samples, table, lut, assign.reshape(1, ROWS))
     refined = refine(residual, codebook[0])
-    return residual, refined[None]
+    return residual, refined.astype(f32)[None]
 
 
 def solution(mesh):

time: 179 us -> 164 us (0.916)
  Pallas kernels: 170 us -> 157 us
  local copies, waits for them, and re-layouts: 6.07 us -> 3.72 us
  other arithmetic: 1.12 us -> 3.29 us
    pallas_call x1, Pallas kernels: 107 us -> 94.4 us  [refine(): pl.pallas_call(em_kernel, out_shape=jax.ShapeDtypeStruct((K, SUB), bf16),...]
    unnamed x12 -> x11, local copies, waits for them, and re-layouts: 5.63 us -> 3.28 us
    broadcast_in_dim x0 -> x1, other arithmetic: none -> 2.17 us  [on_device(): return (residual, refined.astype(f32)[None])]
where the time goes in v2:
time: 164 us
  Pallas kernels  157 us (96%)
  local copies, waits for them, and re-layouts  3.72 us (2%)
  other arithmetic  3.29 us (2%)
    pallas_call x1, Pallas kernels, refine(): pl.pallas_call(em_kernel, out_shape=jax.ShapeDtypeStruct((K, SUB), bf16),...  94.4 us
    pallas_call x1, Pallas kernels, exchange(): pl.pallas_call(exchange_kernel, out_shape=jax.ShapeDtypeStruct((ROWS, SUB...  62.1 us

profile of v2, /device:TPU:2, one launch (start us, length us, event | category | flops | bytes accessed | tf_op | source)
XLA Modules:
  0.0 164.2 jit_solution(12128250426009857229)
XLA Ops:
  0.6 1.1 fusion
  1.7 0.0 copy-start.4
  1.7 0.0 copy-start.2
  1.8 0.1 copy.9
  1.9 0.1 copy.10
  2.0 0.8 copy-done.4
  2.8 0.0 copy-start.3
  2.8 0.2 copy.8
  3.0 0.1 copy-done.2
  3.1 0.4 copy-done.3
  3.6 62.1 %exchange.1.rows = bf16[4096,128]{1,0:T(8,128)(2,1)S(1)} custom-call(bf16[512,1024]{1,0:T(8,128)(2,1)S(1)} %copy-done.2, bf16[2,128,1024]{2,1,0:T(8,128)(2,1)S(1)} %bitcast.13, bf16[256,512]{1,0:T(8,128)(2,1)S(1)} %pad_maximum_fusion.lut, s32[1,4096]{1,0:T(1,128)S(1)} %bitcast.14), custom_call_target="tpu_custom_call" | custom-call | tf_op jit(solution)/shard_map/exchange/pallas_call | solution.py:474
  65.7 0.0 copy-start
  65.7 1.0 copy-done
  66.7 94.4 %refine.1 = bf16[2048,128]{1,0:T(8,128)(2,1)} custom-call(bf16[4096,128]{1,0:T(8,128)(2,1)} %copy-done, f32[2048,128]{1,0:T(8,128)} %bitcast.15), custom_call_target="tpu_custom_call" | custom-call | tf_op jit(solution)/shard_map/refine/pallas_call | solution.py:503
  161.1 0.0 copy-start.1
  161.1 2.2 %bitcast_convert_fusion = f32[1,2048,128]{2,1,0:T(8,128)} fusion(bf16[2048,128]{1,0:T(8,128)(2,1)} %refine.1), kind=kLoop, calls=%fused_computation | loop fusion | flops 262144 | bytes 1572864 | tf_op jit(solution)/shard_map/broadcast_in_dim | solution.py:545
  163.3 0.0 copy-done.1
  163.3 1.0 copy.12
  (1 shorter events, 0.0 us)
Async XLA Ops:
  1.7 1.0 copy-start.4
  1.7 1.4 copy-start.2
  2.8 0.8 copy-start.3
  65.7 1.0 copy-start
  161.1 2.2 %copy-start.1 = (bf16[4096,128]{1,0:T(8,128)(2,1)S(1)}, bf16[4096,128]{1,0:T(8,128)(2,1)}, u32[]{:S(2)}) copy-start(bf16[4096,128]{1,0:T(8,128)(2,1)} %copy-done) | copy-start | bytes 3145732

commit v3 on v2

--- a/solution.py
+++ b/solution.py
@@ -102,6 +102,16 @@
         c = copy(samples.at[:, there], samp.at[here], s_send.at[d - 1], s_recv.at[d - 1], npeers[d - 1])
         c.start()
         s_copies.append(c)
+
+    def forward(i):
+        up(i).wait_recv()
+        if i + 2 <= 6:
+            up(i + 2).start()
+        down(i).wait_recv()
+        if i == 5:
+            down(6).start()
+        elif i + 2 <= 5:
+            down(i + 2).start()
 
     upper[...] = hot(iota((BLK, BLK), 0) < iota((BLK, BLK), 1))
     picked[...] = jnp.zeros_like(picked)
@@ -129,7 +139,9 @@
         picked[...] += nt(parts, hot(iota((CAP, BLK), 0) == rank))
         return carry + jnp.sum(member, axis=1, keepdims=True)
 
-    lax.fori_loop(0, ROWS // BLK, prep, jnp.zeros((NW, 1), f32))
+    carry = lax.fori_loop(0, ROWS // BLK - 2, prep, jnp.zeros((NW, 1), f32))
+    forward(0)
+    lax.fori_loop(ROWS // BLK - 2, ROWS // BLK, prep, carry)
     slots = (picked[:NW] * 256.0 + picked[NW:]).astype(i32)
     for d in range(NX):
         req[d] = slots[d * NZ : (d + 1) * NZ]
@@ -141,6 +153,7 @@
         q_copies.append(c)
     reqin[x] = req[x]
     own_tab.wait()
+    forward(1)
     for c in q_copies:
         c.wait()
 
@@ -198,24 +211,13 @@
 
         lax.fori_loop(0, ROWS // BLK, place, 0)
 
-    due = {1: (0, 1), 2: (2,), 3: (3,), 4: (4,), 5: (5,), 7: (6,)}
-
-    def forward(i):
-        up(i).wait_recv()
-        if i + 2 <= 6:
-            up(i + 2).start()
-        down(i).wait_recv()
-        if i == 5:
-            down(6).start()
-        elif i + 2 <= 5:
-            down(i + 2).start()
+    due = {2: 2, 3: 3, 4: 4, 5: 5, 7: 6}
 
     def step(j, _):
         for when, which in due.items():
             @pl.when(j == when)
             def _():
-                for i in which:
-                    forward(i)
+                forward(which)
 
         gather(j)
 
@@ -413,45 +415,66 @@
             flat = jnp.sum(jnp.where(spot, half, 0.0), axis=0, keepdims=True)
             norm[...] = jnp.where(iota((8, SUB), 0) == z // 2, flat, 0.0)
 
-        sends = []
+        def block_at(xx, d):
+            zz = lax.rem(z - d + NZ, NZ)
+            return fresh.at[it, pl.ds(pl.multiple_of(xx * XK + zz * OWN, OWN), OWN)]
+
+        def spread(d, q, src, dev):
+            a = copy(src, src, ax_send.at[it, d, q], ax_recv.at[it, d, q], dev)
+            a.start()
+            return a
+
+        over_z, norms, over_x, relays = {}, [], {}, []
         for d in (4, 3, 5, 2, 6, 1, 7):
-            src = fresh.at[it, pl.ds(first, OWN)]
-            a = copy(src, src, az_send.at[it, d - 1], az_recv.at[it, d - 1], zpeers[d - 1])
-            a.start()
-            sends.append(a)
-            if not last:
+            src = block_at(x, 0)
+            over_z[d] = copy(src, src, az_send.at[it, d - 1], az_recv.at[it, d - 1], zpeers[d - 1])
+            over_z[d].start()
+        if not last:
+            for d in (4, 3, 5, 2, 6, 1, 7):
                 e = copy(norm, normx.at[NX + d - 1], an_send.at[d - 1], an_recv.at[d - 1], zpeers[d - 1])
                 e.start()
-                sends.append(e)
-        for s in sends:
-            s.wait_recv()
-        pending += sends
+                norms.append(e)
+
+        def relay(d):
+            over_x[d][d % 2].wait_recv()
+            if d % 2 == 0:
+                relays.append(spread(d, 2, block_at(lax.rem(x + 3, NX), d), right))
+            else:
+                relays.append(spread(d, 2, block_at(lax.rem(x + 1, NX), d), left))
+
+        order = (0, 1, 7, 2, 6, 3, 5, 4)
+        for at, d in enumerate(order):
+            if d:
+                over_z[d].wait_recv()
+            src = block_at(x, d)
+            over_x[d] = (spread(d, 0, src, right), spread(d, 1, src, left))
+            if at >= 3:
+                relay(order[at - 3])
         if not last:
             mine = norm[...]
+            for d, e in enumerate(norms):
+                e.wait_recv()
             for d in range(NZ - 1):
                 mine = mine + normx[NX + d]
             normx[x] = mine
-        def spread(q, xx, h, dev):
-            src = fresh.at[it, pl.ds(pl.multiple_of(xx * XK + h * XH, XH), XH)]
-            a = copy(src, src, ax_send.at[it, q], ax_recv.at[it, q], dev)
-            a.start()
-            return a
-
-        sends = [spread(0, x, 0, right), spread(1, x, 1, left)]
-        if not last:
+            norms_x = []
             for d in (2, 1, 3):
                 e = copy(normx.at[x], normx.at[x], am_send.at[d - 1], am_recv.at[d - 1], xpeers[d - 1])
                 e.start()
-                sends.append(e)
-        sends += [spread(2, x, 1, right), spread(3, x, 0, left)]
-        sends[0].wait_recv()
-        relay = [spread(4, lax.rem(x + 3, NX), 0, right)]
-        sends[1].wait_recv()
-        relay.append(spread(5, lax.rem(x + 1, NX), 1, left))
-        sends = sends + relay
-        for s in sends[2:]:
-            s.wait_recv()
-        pending += sends
+                norms_x.append(e)
+        for d in order[-3:]:
+            relay(d)
+        for d in order:
+            over_x[d][1 - d % 2].wait_recv()
+        for e in relays:
+            e.wait_recv()
+        pending += list(over_z.values()) + norms + relays
+        for pair_of in over_x.values():
+            pending += list(pair_of)
+        if not last:
+            for e in norms_x:
+                e.wait_recv()
+            pending += norms_x
         if last:
             out[...] = fresh[it]
         else:
@@ -527,7 +550,7 @@
             pltpu.VMEM((NX + 7, 8, SUB), f32),
             pltpu.VMEM((OWN, SUB), f32),
             dma(x6), dma(x6), dma(x3), dma(x3), dma(z7), dma(z7), dma(z7), dma(z7),
-            dma(z7), dma(z7), dma((7,)), dma((7,)), dma(x6), dma(x6), dma((3,)), dma((3,)),
+            dma(z7), dma(z7), dma((7,)), dma((7,)), dma((ITERS, NZ, 3)), dma((ITERS, NZ, 3)), dma((3,)), dma((3,)),
         ],
         compiler_params=pltpu.CompilerParams(
             collective_id=1, has_side_effects=True, vmem_limit_bytes=56 << 20

time: 164 us -> 169 us (1.030)
  Pallas kernels: 157 us -> 161 us
    pallas_call x1, Pallas kernels: 94.4 us -> 98.6 us  [refine(): pl.pallas_call(em_kernel, out_shape=jax.ShapeDtypeStruct((K, SUB), bf16),...]
where the time goes in v3:
time: 169 us; the launch traced here: 168 us
  Pallas kernels  161 us (95%)
  local copies, waits for them, and re-layouts  3.72 us (2%)
  other arithmetic  3.29 us (2%)
    pallas_call x1, Pallas kernels, refine(): pl.pallas_call(em_kernel, out_shape=jax.ShapeDtypeStruct((K, SUB), bf16),...  98.6 us
    pallas_call x1, Pallas kernels, exchange(): pl.pallas_call(exchange_kernel, out_shape=jax.ShapeDtypeStruct((ROWS, SUB...  62.1 us

profile of v3, /device:TPU:2, one launch (start us, length us, event | category | flops | bytes accessed | tf_op | source)
XLA Modules:
  0.0 168.4 jit_solution(9815733615750034523)
XLA Ops:
  0.6 1.1 fusion
  1.7 0.0 copy-start.4
  1.7 0.0 copy-start.2
  1.8 0.1 copy.9
  1.9 0.1 copy.10
  2.0 0.8 copy-done.4
  2.8 0.0 copy-start.3
  2.8 0.2 copy.8
  3.0 0.1 copy-done.2
  3.1 0.4 copy-done.3
  3.6 62.1 %exchange.1.rows = bf16[4096,128]{1,0:T(8,128)(2,1)S(1)} custom-call(bf16[512,1024]{1,0:T(8,128)(2,1)S(1)} %copy-done.2, bf16[2,128,1024]{2,1,0:T(8,128)(2,1)S(1)} %bitcast.13, bf16[256,512]{1,0:T(8,128)(2,1)S(1)} %pad_maximum_fusion.lut, s32[1,4096]{1,0:T(1,128)S(1)} %bitcast.14), custom_call_target="tpu_custom_call" | custom-call | tf_op jit(solution)/shard_map/exchange/pallas_call | solution.py:497
  65.7 0.0 copy-start
  65.7 1.0 copy-done
  66.7 98.6 %refine.1 = bf16[2048,128]{1,0:T(8,128)(2,1)} custom-call(bf16[4096,128]{1,0:T(8,128)(2,1)} %copy-done, f32[2048,128]{1,0:T(8,128)} %bitcast.15), custom_call_target="tpu_custom_call" | custom-call | tf_op jit(solution)/shard_map/refine/pallas_call | solution.py:526
  165.3 0.0 copy-start.1
  165.3 2.2 %bitcast_convert_fusion = f32[1,2048,128]{2,1,0:T(8,128)} fusion(bf16[2048,128]{1,0:T(8,128)(2,1)} %refine.1), kind=kLoop, calls=%fused_computation | loop fusion | flops 262144 | bytes 1572864 | tf_op jit(solution)/shard_map/broadcast_in_dim | solution.py:568
  167.5 0.0 copy-done.1
  167.5 1.0 copy.12
  (1 shorter events, 0.0 us)
Async XLA Ops:
  1.7 1.0 copy-start.4
  1.7 1.4 copy-start.2
  2.8 0.8 copy-start.3
  65.7 1.0 copy-start
  165.3 2.2 %copy-start.1 = (bf16[4096,128]{1,0:T(8,128)(2,1)S(1)}, bf16[4096,128]{1,0:T(8,128)(2,1)}, u32[]{:S(2)}) copy-start(bf16[4096,128]{1,0:T(8,128)(2,1)} %copy-done) | copy-start | bytes 3145732

commit v4 on v2

--- a/solution.py
+++ b/solution.py
@@ -250,15 +250,16 @@
 RB = 512
 KC = 256
 XH = XK // 2
+TAIL = 16
+BOX = OWN + TAIL
 SCALE = math.log2(math.e) / 8.0
 
 
 def em_kernel(
     rows, book, out,
     aug, scaled, words, probs, score, score2,
-    xs, keep, xc, xin, xcin, zs, zc, zin, zcin, fresh, norm, normz, normx, own,
-    x_send, x_recv, xc_send, xc_recv, z_send, z_recv, zc_send, zc_recv,
-    az_send, az_recv, an_send, an_recv, ax_send, ax_recv, am_send, am_recv,
+    xs, keep, xin, zs, zin, fresh, line_of, own,
+    x_send, x_recv, z_send, z_recv, az_send, az_recv, ax_send, ax_recv,
 ):
     w = lax.axis_index("wide")
     z = w // NX
@@ -342,108 +343,103 @@
             c = t[:, SUB : SUB + 1] + t[:, SUB + 1 : SUB + 2]
             spread = jnp.where(iota((XK, SUB), 1) == lax.rem(iota((XK, SUB), 0), SUB), c, 0.0)
             c = jnp.sum(spread.reshape(XK // SUB, SUB, SUB), axis=1)
-            return t[:, :SUB], jnp.concatenate([c, jnp.zeros_like(c)], axis=0)
+            return t[:, :SUB], c
 
         right, across, left = xpeers
 
-        def tell(d, c):
-            xc[it, d - 1] = c
-            e = copy(xc.at[it, d - 1], xcin.at[it, d - 1], xc_send.at[it, d - 1], xc_recv.at[it, d - 1], xpeers[d - 1])
-            e.start()
-            return e
-
-        def part_to(q, value, dev):
-            xs[it, q] = value.astype(bf16)
+        def tail_of(c):
+            hi = c.astype(bf16).astype(f32)
+            rest = jnp.zeros((TAIL - 2 * c.shape[0], SUB), f32)
+            return jnp.concatenate([hi, c - hi, rest], axis=0).astype(bf16)
+
+        def part_to(q, value, c, dev):
+            xs[it, q, :XH] = value.astype(bf16)
+            xs[it, q, XH:] = tail_of(c)
             a = copy(xs.at[it, q], xin.at[it, q], x_send.at[it, q], x_recv.at[it, q], dev)
             a.start()
             return a
 
+        def got(q):
+            c = xin[it, q, XH:].astype(f32)
+            return xin[it, q, :XH].astype(f32), c[0:2] + c[2:4]
+
         t, c = chunk(lax.rem(x + 2, NX))
-        sends = [part_to(0, t[:XH], right), part_to(1, t[XH:], left), tell(2, c)]
+        sends = [part_to(0, t[:XH], c[:2], right), part_to(1, t[XH:], c[2:], left)]
         t, c = chunk(lax.rem(x + 1, NX))
-        sends += [part_to(2, t[XH:], right), tell(1, c)]
+        sends.append(part_to(2, t[XH:], c[2:], right))
         keep[:XH] = t[:XH]
+        ahead_c = c[:2]
         t, c = chunk(lax.rem(x + 3, NX))
-        sends += [part_to(3, t[:XH], left), tell(3, c)]
+        sends.append(part_to(3, t[:XH], c[:2], left))
         keep[XH:] = t[XH:]
+        behind_c = c[2:]
         sends[0].wait_recv()
-        relay = [part_to(4, keep[:XH] + xin[it, 0].astype(f32), right)]
+        t, c = got(0)
+        relay = [part_to(4, keep[:XH] + t, ahead_c + c, right)]
         sends[1].wait_recv()
-        relay.append(part_to(5, keep[XH:] + xin[it, 1].astype(f32), left))
+        t, c = got(1)
+        relay.append(part_to(5, keep[XH:] + t, behind_c + c, left))
         total, count = chunk(x)
         for s in sends[2:] + relay:
             s.wait_recv()
-        total = total + jnp.concatenate(
-            [xin[it, 4].astype(f32) + xin[it, 3].astype(f32),
-             xin[it, 5].astype(f32) + xin[it, 2].astype(f32)], axis=0)
-        for d in range(3):
-            count = count + xcin[it, d]
-        sends += relay
-        zs[it] = total.astype(bf16)
+        (t4, c4), (t3, c3), (t5, c5), (t2, c2) = got(4), got(3), got(5), got(2)
+        total = total + jnp.concatenate([t4 + t3, t5 + t2], axis=0)
+        count = count + jnp.concatenate([c4 + c3, c5 + c2], axis=0)
+        pending += sends + relay
+        tail = tail_of(count)
+        for zz in range(NZ):
+            zs[it, zz, :OWN] = total[zz * OWN : (zz + 1) * OWN].astype(bf16)
+            zs[it, zz, OWN:] = tail
         score[pl.ds(0, XK), :SUB] = total
-        zc[it] = count
-        pending += sends
 
         sends = []
         for d in (4, 3, 5, 2, 6, 1, 7):
             zz = lax.rem(z + d, NZ)
-            a = copy(zs.at[it, pl.ds(pl.multiple_of(zz * OWN, OWN), OWN)], zin.at[it, d - 1],
-                     z_send.at[it, d - 1], z_recv.at[it, d - 1], zpeers[d - 1])
-            e = copy(zc.at[it], zcin.at[it, d - 1], zc_send.at[it, d - 1], zc_recv.at[it, d - 1], zpeers[d - 1])
+            a = copy(zs.at[it, zz], zin.at[it, d - 1], z_send.at[it, d - 1], z_recv.at[it, d - 1], zpeers[d - 1])
             a.start()
-            e.start()
-            sends += [a, e]
+            sends.append(a)
         part = score[pl.ds(pl.multiple_of(z * OWN, OWN), OWN), :SUB]
         for s in sends:
             s.wait_recv()
         for d in range(NZ - 1):
-            part = part + zin[it, d].astype(f32)
-            count = count + zcin[it, d]
+            part = part + zin[it, d, :OWN].astype(f32)
+            c = zin[it, d, OWN:].astype(f32)
+            count = count + (c[0:4] + c[4:8])
         pending += sends
-        normz[...] = count
-        line = normz[pl.ds(z // 2, 1), :]
+        line_of[...] = jnp.concatenate([count, count], axis=0)
+        line = line_of[pl.ds(z // 2, 1), :]
         spot = iota((OWN, SUB), 1) == iota((OWN, SUB), 0) + lax.rem(z, 2) * OWN
         cnt = jnp.sum(jnp.where(spot, jnp.broadcast_to(line, (OWN, SUB)), 0.0), axis=1, keepdims=True)
         new = (part + own[...]) / (cnt + 1.0)
         own[...] = new
-        fresh[it, pl.ds(first, OWN), :] = new.astype(bf16)
+        half = -0.5 * jnp.sum(new * new, axis=1, keepdims=True)
+        flat = jnp.sum(jnp.where(spot, half, 0.0), axis=0, keepdims=True)
+        hi = flat.astype(bf16).astype(f32)
+        mid = (flat - hi).astype(bf16).astype(f32)
+        row = iota((TAIL, SUB), 0)
+        fresh[it, x, z, :OWN] = new.astype(bf16)
+        fresh[it, x, z, OWN:] = jnp.where(
+            row == 0, hi, jnp.where(row == 1, mid, jnp.where(row == 2, flat - hi - mid, 0.0))
+        ).astype(bf16)
         last = it == ITERS - 1
-        if not last:
-            half = -0.5 * jnp.sum(new * new, axis=1, keepdims=True)
-            flat = jnp.sum(jnp.where(spot, half, 0.0), axis=0, keepdims=True)
-            norm[...] = jnp.where(iota((8, SUB), 0) == z // 2, flat, 0.0)
 
         sends = []
         for d in (4, 3, 5, 2, 6, 1, 7):
-            src = fresh.at[it, pl.ds(first, OWN)]
+            src = fresh.at[it, x, z]
             a = copy(src, src, az_send.at[it, d - 1], az_recv.at[it, d - 1], zpeers[d - 1])
             a.start()
             sends.append(a)
-            if not last:
-                e = copy(norm, normx.at[NX + d - 1], an_send.at[d - 1], an_recv.at[d - 1], zpeers[d - 1])
-                e.start()
-                sends.append(e)
         for s in sends:
             s.wait_recv()
         pending += sends
-        if not last:
-            mine = norm[...]
-            for d in range(NZ - 1):
-                mine = mine + normx[NX + d]
-            normx[x] = mine
+
         def spread(q, xx, h, dev):
-            src = fresh.at[it, pl.ds(pl.multiple_of(xx * XK + h * XH, XH), XH)]
+            src = fresh.at[it, xx, pl.ds(h * (NZ // 2), NZ // 2)]
             a = copy(src, src, ax_send.at[it, q], ax_recv.at[it, q], dev)
             a.start()
             return a
 
-        sends = [spread(0, x, 0, right), spread(1, x, 1, left)]
-        if not last:
-            for d in (2, 1, 3):
-                e = copy(normx.at[x], normx.at[x], am_send.at[d - 1], am_recv.at[d - 1], xpeers[d - 1])
-                e.start()
-                sends.append(e)
-        sends += [spread(2, x, 1, right), spread(3, x, 0, left)]
+        sends = [spread(0, x, 0, right), spread(1, x, 1, left), spread(2, x, 1, right), spread(3, x, 0, left)]
         sends[0].wait_recv()
         relay = [spread(4, lax.rem(x + 3, NX), 0, right)]
         sends[1].wait_recv()
@@ -452,15 +448,17 @@
         for s in sends[2:]:
             s.wait_recv()
         pending += sends
-        if last:
-            out[...] = fresh[it]
-        else:
-            words[:, :SUB] = fresh[it]
-            for xx in range(NX):
-                for q in range(XK // SUB):
-                    at = pl.ds(xx * XK + q * SUB, SUB)
-                    half = jnp.broadcast_to(normx[xx, q : q + 1, :], (SUB, SUB)).T
-                    words[at, SUB:] = extra(half).astype(bf16)
+        for xx in range(NX):
+            for q in range(XK // SUB):
+                at = pl.ds(xx * XK + q * SUB, SUB)
+                pair_rows = jnp.concatenate([fresh[it, xx, 2 * q, :OWN], fresh[it, xx, 2 * q + 1, :OWN]], axis=0)
+                if last:
+                    out[at, :] = pair_rows
+                else:
+                    words[at, :SUB] = pair_rows
+                    c = fresh[it, xx, 2 * q, OWN:].astype(f32) + fresh[it, xx, 2 * q + 1, OWN:].astype(f32)
+                    flat = c[0:1] + (c[1:2] + c[2:3])
+                    words[at, SUB:] = extra(jnp.broadcast_to(flat, (SUB, SUB)).T).astype(bf16)
     for s in pending:
         s.wait_send()
 
@@ -499,7 +497,7 @@
 
 def refine(rows, book):
     dma = pltpu.SemaphoreType.DMA
-    x3, z7, x6 = (ITERS, 3), (ITERS, 7), (ITERS, 6)
+    z7, x6 = (ITERS, 7), (ITERS, 6)
     return pl.pallas_call(
         em_kernel,
         out_shape=jax.ShapeDtypeStruct((K, SUB), bf16),
@@ -512,22 +510,15 @@
             pltpu.VMEM((K, ROWS), bf16),
             pltpu.VMEM((K, RB), f32),
             pltpu.VMEM((K, RB), f32),
-            pltpu.VMEM((ITERS, 6, XH, SUB), bf16),
+            pltpu.VMEM((ITERS, 6, XH + TAIL, SUB), bf16),
             pltpu.VMEM((XK, SUB), f32),
-            pltpu.VMEM((ITERS, 3, 8, SUB), f32),
-            pltpu.VMEM((ITERS, 6, XH, SUB), bf16),
-            pltpu.VMEM((ITERS, 3, 8, SUB), f32),
-            pltpu.VMEM((ITERS, XK, SUB), bf16),
-            pltpu.VMEM((ITERS, 8, SUB), f32),
-            pltpu.VMEM((ITERS, 7, OWN, SUB), bf16),
-            pltpu.VMEM((ITERS, 7, 8, SUB), f32),
-            pltpu.VMEM((ITERS, K, SUB), bf16),
+            pltpu.VMEM((ITERS, 6, XH + TAIL, SUB), bf16),
+            pltpu.VMEM((ITERS, NZ, BOX, SUB), bf16),
+            pltpu.VMEM((ITERS, NZ - 1, BOX, SUB), bf16),
+            pltpu.VMEM((ITERS, NX, NZ, BOX, SUB), bf16),
             pltpu.VMEM((8, SUB), f32),
-            pltpu.VMEM((8, SUB), f32),
-            pltpu.VMEM((NX + 7, 8, SUB), f32),
             pltpu.VMEM((OWN, SUB), f32),
-            dma(x6), dma(x6), dma(x3), dma(x3), dma(z7), dma(z7), dma(z7), dma(z7),
-            dma(z7), dma(z7), dma((7,)), dma((7,)), dma(x6), dma(x6), dma((3,)), dma((3,)),
+            dma(x6), dma(x6), dma(z7), dma(z7), dma(z7), dma(z7), dma(x6), dma(x6),
         ],
         compiler_params=pltpu.CompilerParams(
             collective_id=1, has_side_effects=True, vmem_limit_bytes=56 << 20

time: 164 us -> 165 us (level)
  no operation moved by 1% of the time
where the time goes in v4:
time: 165 us
  Pallas kernels  157 us (95%)
  local copies, waits for them, and re-layouts  3.72 us (2%)
  other arithmetic  3.29 us (2%)
    pallas_call x1, Pallas kernels, refine(): pl.pallas_call(em_kernel, out_shape=jax.ShapeDtypeStruct((K, SUB), bf16),...  94.8 us
    pallas_call x1, Pallas kernels, exchange(): pl.pallas_call(exchange_kernel, out_shape=jax.ShapeDtypeStruct((ROWS, SUB...  62.1 us

profile of v4, /device:TPU:2, one launch (start us, length us, event | category | flops | bytes accessed | tf_op | source)
XLA Modules:
  0.0 164.6 jit_solution(13161040949814103379)
XLA Ops:
  0.6 1.1 fusion
  1.7 0.0 copy-start.4
  1.7 0.0 copy-start.2
  1.8 0.1 copy.9
  1.9 0.1 copy.10
  2.0 0.8 copy-done.4
  2.8 0.0 copy-start.3
  2.8 0.2 copy.8
  3.0 0.1 copy-done.2
  3.1 0.4 copy-done.3
  3.6 62.1 %exchange.1.rows = bf16[4096,128]{1,0:T(8,128)(2,1)S(1)} custom-call(bf16[512,1024]{1,0:T(8,128)(2,1)S(1)} %copy-done.2, bf16[2,128,1024]{2,1,0:T(8,128)(2,1)S(1)} %bitcast.13, bf16[256,512]{1,0:T(8,128)(2,1)S(1)} %pad_maximum_fusion.lut, s32[1,4096]{1,0:T(1,128)S(1)} %bitcast.14), custom_call_target="tpu_custom_call" | custom-call | tf_op jit(solution)/shard_map/exchange/pallas_call | solution.py:472
  65.7 0.0 copy-start
  65.7 1.0 copy-done
  66.7 94.8 %refine.1 = bf16[2048,128]{1,0:T(8,128)(2,1)} custom-call(bf16[4096,128]{1,0:T(8,128)(2,1)} %copy-done, f32[2048,128]{1,0:T(8,128)} %bitcast.15), custom_call_target="tpu_custom_call" | custom-call | tf_op jit(solution)/shard_map/refine/pallas_call | solution.py:501
  161.5 0.0 copy-start.1
  161.5 2.2 %bitcast_convert_fusion = f32[1,2048,128]{2,1,0:T(8,128)} fusion(bf16[2048,128]{1,0:T(8,128)(2,1)} %refine.1), kind=kLoop, calls=%fused_computation | loop fusion | flops 262144 | bytes 1572864 | tf_op jit(solution)/shard_map/broadcast_in_dim | solution.py:536
  163.6 0.0 copy-done.1
  163.6 1.0 copy.12
  (1 shorter events, 0.0 us)
Async XLA Ops:
  1.7 1.0 copy-start.4
  1.7 1.4 copy-start.2
  2.8 0.8 copy-start.3
  65.7 1.0 copy-start
  161.5 2.2 %copy-start.1 = (bf16[4096,128]{1,0:T(8,128)(2,1)S(1)}, bf16[4096,128]{1,0:T(8,128)(2,1)}, u32[]{:S(2)}) copy-start(bf16[4096,128]{1,0:T(8,128)(2,1)} %copy-done) | copy-start | bytes 3145732

commit v5 on v2

--- a/solution.py
+++ b/solution.py
@@ -39,7 +39,7 @@
     barrier = pltpu.get_barrier_semaphore()
     for peer in peers:
         pl.semaphore_signal(barrier, inc=1, device_id=peer, device_id_type=MESH)
-    pl.semaphore_wait(barrier, len(peers))
+    return lambda: pl.semaphore_wait(barrier, len(peers))
 
 
 def exchange_kernel(
@@ -59,7 +59,11 @@
     xpeers = [at_zx(z, x + d) for d in range(1, NX)]
     npeers = [{"narrow": lax.rem(n + d, NN)} for d in range(1, NN)]
     above, below = at_zx(z + 1, x), at_zx(z - 1, x)
-    greet([above, below] + xpeers + npeers)
+    settle = greet([above, below] + xpeers + npeers)
+    upper[...] = hot(iota((BLK, BLK), 0) < iota((BLK, BLK), 1))
+    picked[...] = jnp.zeros_like(picked)
+    centre[...] = jnp.zeros_like(centre)
+    settle()
 
     def copy(src, dst, send, recv, dev):
         return pltpu.make_async_remote_copy(
@@ -102,10 +106,6 @@
         c = copy(samples.at[:, there], samp.at[here], s_send.at[d - 1], s_recv.at[d - 1], npeers[d - 1])
         c.start()
         s_copies.append(c)
-
-    upper[...] = hot(iota((BLK, BLK), 0) < iota((BLK, BLK), 1))
-    picked[...] = jnp.zeros_like(picked)
-    centre[...] = jnp.zeros_like(centre)
 
     def prep(b, carry):
         cols = pl.ds(pl.multiple_of(b * BLK, BLK), BLK)
@@ -265,7 +265,7 @@
     x = lax.rem(w, NX)
     xpeers = [{"wide": z * NX + lax.rem(x + d, NX)} for d in range(1, NX)]
     zpeers = [{"wide": lax.rem(z + d, NZ) * NX + x} for d in range(1, NZ)]
-    greet(xpeers + zpeers)
+    settle = greet(xpeers + zpeers)
 
     def copy(src, dst, send, recv, dev):
         return pltpu.make_async_remote_copy(
@@ -359,6 +359,8 @@
             return a
 
         t, c = chunk(lax.rem(x + 2, NX))
+        if it == 0:
+            settle()
         sends = [part_to(0, t[:XH], right), part_to(1, t[XH:], left), tell(2, c)]
         t, c = chunk(lax.rem(x + 1, NX))
         sends += [part_to(2, t[XH:], right), tell(1, c)]

time: 164 us -> 161 us (0.982)
  Pallas kernels: 157 us -> 153 us
    pallas_call x1, Pallas kernels: 94.4 us -> 90.7 us  [refine(): pl.pallas_call(em_kernel, out_shape=jax.ShapeDtypeStruct((K, SUB), bf16),...]
where the time goes in v5:
time: 161 us
  Pallas kernels  153 us (95%)
  local copies, waits for them, and re-layouts  3.72 us (2%)
  other arithmetic  3.29 us (2%)
    pallas_call x1, Pallas kernels, refine(): pl.pallas_call(em_kernel, out_shape=jax.ShapeDtypeStruct((K, SUB), bf16),...  90.7 us
    pallas_call x1, Pallas kernels, exchange(): pl.pallas_call(exchange_kernel, out_shape=jax.ShapeDtypeStruct((ROWS, SUB...  62.1 us
    unnamed x11, local copies, waits for them, and re-layouts  3.28 us

profile of v5, /device:TPU:2, one launch (start us, length us, event | category | flops | bytes accessed | tf_op | source)
XLA Modules:
  0.0 160.6 jit_solution(7885068060387697933)
XLA Ops:
  0.6 1.1 fusion
  1.7 0.0 copy-start.4
  1.7 0.0 copy-start.2
  1.8 0.1 copy.9
  1.9 0.1 copy.10
  2.0 0.8 copy-done.4
  2.8 0.0 copy-start.3
  2.8 0.2 copy.8
  3.0 0.1 copy-done.2
  3.1 0.4 copy-done.3
  3.6 62.1 %exchange.1.rows = bf16[4096,128]{1,0:T(8,128)(2,1)S(1)} custom-call(bf16[512,1024]{1,0:T(8,128)(2,1)S(1)} %copy-done.2, bf16[2,128,1024]{2,1,0:T(8,128)(2,1)S(1)} %bitcast.13, bf16[256,512]{1,0:T(8,128)(2,1)S(1)} %pad_maximum_fusion.lut, s32[1,4096]{1,0:T(1,128)S(1)} %bitcast.14), custom_call_target="tpu_custom_call" | custom-call | tf_op jit(solution)/shard_map/exchange/pallas_call | solution.py:476
  65.7 0.0 copy-start
  65.7 1.0 copy-done
  66.7 90.7 %refine.1 = bf16[2048,128]{1,0:T(8,128)(2,1)} custom-call(bf16[4096,128]{1,0:T(8,128)(2,1)} %copy-done, f32[2048,128]{1,0:T(8,128)} %bitcast.15), custom_call_target="tpu_custom_call" | custom-call | tf_op jit(solution)/shard_map/refine/pallas_call | solution.py:505
  157.4 0.0 copy-start.1
  157.4 2.2 %bitcast_convert_fusion = f32[1,2048,128]{2,1,0:T(8,128)} fusion(bf16[2048,128]{1,0:T(8,128)(2,1)} %refine.1), kind=kLoop, calls=%fused_computation | loop fusion | flops 262144 | bytes 1572864 | tf_op jit(solution)/shard_map/broadcast_in_dim | solution.py:547
  159.6 0.0 copy-done.1
  159.6 1.0 copy.12
  (1 shorter events, 0.0 us)
Async XLA Ops:
  1.7 1.0 copy-start.4
  1.7 1.4 copy-start.2
  2.8 0.8 copy-start.3
  65.7 1.0 copy-start
  157.4 2.2 %copy-start.1 = (bf16[4096,128]{1,0:T(8,128)(2,1)S(1)}, bf16[4096,128]{1,0:T(8,128)(2,1)}, u32[]{:S(2)}) copy-start(bf16[4096,128]{1,0:T(8,128)(2,1)} %copy-done) | copy-start | bytes 3145732
